TPU v7x, 32 devices: a whole 2x2x4 slice. The times are simulated.
32 devices in a mesh: prompt: 2 (over y), tensor: 4 (over z), ctx: 4 (over x, core).
Axes of the slice: x: 2, y: 2, z: 4, core: 2. Of those that a mesh axis runs over, the one named last changes fastest.
Arguments:
- hidden_in: bfloat16 [2048, 8192], P(('prompt', 'ctx', 'tensor')), parts along dimension 0, may hold values from -6 to 6
- norm_gain: float32 [8192], replicated, may hold values from 0.1 to 1.9
- weight_in: bfloat16 [8192, 3, 4096], P('ctx', None, 'tensor'), may hold values from -0.0625 to 0.0625
- filter_taps: float32 [256, 128], P('tensor'), may hold values from -0.6 to 0.6
- filter_decay: float32 [256], P('tensor'), may hold values from 0.003 to 0.3
- skip_gain: float32 [4096], P('tensor'), may hold values from -1 to 1
- tail_cache: bfloat16 [254, 4096], P('prompt', 'tensor'), parts along dimension 0, may hold values from -6 to 6
- output_weight: bfloat16 [4096, 8192], P(None, 'tensor'), may hold values from -0.09375 to 0.09375
Outputs:
- mixer_output: bfloat16 [2048, 8192], P(('prompt', 'ctx'), 'tensor'), parts along dimension 0
There are 2 independent parts, one for each index of `prompt`. A program takes and returns all parts, laid end to end along the dimension named above; an argument that names none is the same for every part. Nothing has to cross between parts.
All inputs are finite; a program needn't handle non-finite values.
Results may differ from a plain program's by a relative error of at most 0.0095.
Values may be sent and summed in bfloat16 or wider, within the bound.
A program may use at most 256 MiB of HBM per device.

v0:
```python
import jax
import jax.numpy as jnp
from jax import lax
from jax.sharding import PartitionSpec as P

GROUP = 16


def passed_along(value, axis, steps):
    count = lax.axis_size(axis)
    leading, last = (max(0, -steps), min(count, count - steps))
    return lax.ppermute(value, axis, [(source, source + steps) for source in range(leading, last)])


def normalize_rows(hidden_in, norm_gain):
    values = hidden_in.astype(jnp.float32)
    scaled = lax.rsqrt(jnp.mean(values * values, axis=-1, keepdims=True) + 1e-06)
    return (values * scaled * norm_gain[None, :]).astype(jnp.bfloat16)


def banded_taps(taps_full, shard_rows):
    group_count, tap_count = taps_full.shape
    width = shard_rows + tap_count - 1
    first_row = jnp.concatenate(
        [taps_full[:, ::-1], jnp.zeros((group_count, width + 1 - tap_count), jnp.float32)], axis=1
    )
    repeated = jnp.tile(first_row, (1, shard_rows))
    return repeated[:, : shard_rows * width].reshape(group_count, shard_rows, width)


def on_device(
    hidden_in, norm_gain, weight_in, filter_taps, filter_decay, skip_gain, tail_cache, output_weight
):
    gathered = lax.all_gather(hidden_in, "tensor", axis=0, tiled=True)
    normed = normalize_rows(gathered, norm_gain)
    shard_rows = normed.shape[0]
    channels = weight_in.shape[2]
    qkv = jnp.einsum(
        "td,dgc->tgc",
        normed,
        lax.all_gather(weight_in, "ctx", axis=0, tiled=True),
        preferred_element_type=jnp.float32,
    )
    query = qkv[:, 0]
    product = (qkv[:, 1] * qkv[:, 2]).astype(jnp.bfloat16)
    tail_rows = filter_taps.shape[1] - 1
    incoming = passed_along(product[shard_rows - tail_rows :], "ctx", 1)
    leading = lax.axis_index("ctx") == 0
    before = jnp.where(leading, tail_cache, incoming)
    extended = jnp.concatenate([before, product], axis=0).astype(jnp.float32)
    lags = jnp.arange(filter_taps.shape[1]).astype(jnp.float32)
    taps_full = filter_taps * jnp.exp(-filter_decay[:, None] * lags[None, :])
    band = banded_taps(taps_full, shard_rows)
    group_count = taps_full.shape[0]
    grouped = extended.reshape(extended.shape[0], group_count, GROUP)
    filtered = jnp.einsum(
        "gsj,jgi->sgi",
        band,
        grouped,
        precision=lax.Precision.HIGHEST,
        preferred_element_type=jnp.float32,
    ).reshape(shard_rows, channels)
    gated = (query * (filtered + skip_gain[None, :] * product.astype(jnp.float32))).astype(
        jnp.bfloat16
    )
    totals = jnp.dot(
        lax.all_gather(gated, "tensor", axis=1, tiled=True),
        output_weight,
        preferred_element_type=jnp.float32,
    )
    return totals.astype(jnp.bfloat16)


def solution(mesh):
    in_specs = (
        P(("prompt", "ctx", "tensor"), None),
        P(),
        P("ctx", None, "tensor"),
        P("tensor", None),
        P("tensor"),
        P("tensor"),
        P("prompt", "tensor"),
        P(None, "tensor"),
    )
    out_specs = P(("prompt", "ctx"), "tensor")
    return jax.shard_map(
        on_device, mesh=mesh, in_specs=in_specs, out_specs=out_specs, check_vma=False
    )
```

profile of v0, /device:TPU:0, one launch (start us, length us, event | category | flops | bytes accessed | tf_op | source)
XLA Modules:
  0.0 509.6 jit_solution(4066531910178312621)
XLA Ops:
  6.5 0.0 copy-start.4
  6.5 0.0 copy-start.1
  6.5 0.0 all-gather.4.cloned.1.call-start
  6.5 0.7 all-gather.4.cloned.1.call-update
  7.3 0.0 all-gather.6.cloned.1.call-start
  7.3 0.7 all-gather.6.cloned.1.call-update
  8.0 0.0 all-gather.8.cloned.1.call-start
  8.1 0.0 copy-done.4
  8.1 0.0 copy-done.1
  8.1 0.1 exponential_multiply_fusion
  8.2 0.1 rev.3
  8.3 10.3 %tile.4 = f32[64,256,384]{2,1,0:T(8,128)} broadcast(f32[64,384]{1,0:T(8,128)S(1)} %concatenate.7), dimensions={0,2} | broadcast | bytes 25264128 | tf_op jit(solution)/shard_map/tile | solution.py:27
  18.6 22.1 %copy.13 = f32[8,8,256,384]{3,1,2,0:T(8,128)S(1)} copy(f32[8,8,256,384]{3,2,1,0:T(8,128)} %bitcast.25) | data formatting | bytes 50331648
  40.7 8.6 %slice.28 = f32[64,98048]{1,0:T(8,128)} slice(f32[64,98304]{1,0:T(8,128)S(1)} %bitcast.26), slice={[0:64], [0:98048]} | slice | bytes 50200576 | tf_op jit(solution)/shard_map/slice | solution.py:28
  49.3 0.0 copy-start.3
  49.3 32.8 %reshape.33 = f32[64,256,383]{2,1,0:T(8,128)} reshape(f32[64,98048]{1,0:T(8,128)} %slice.28) | data formatting | bytes 50200576 | tf_op jit(solution)/shard_map/reshape | solution.py:28
  82.1 10.3 %all-gather.4.cloned.1.call-done = bf16[256,8192]{1,0:T(8,128)(2,1)} async-done(((bf16[64,8192]{1,0:T(8,128)(2,1)}), bf16[256,8192]{1,0:T(8,128)(2,1)}) %all-gather.4.cloned.1.call-update) | async-done | bytes 4194320 | tf_op jit(solution)/shard_map/all_gather | solution.py:34
  92.4 3.1 fusion
  95.5 0.0 copy-start
  95.5 294.1 %all-gather.6.cloned.1.call-done = bf16[8192,3,1024]{2,0,1:T(8,128)(2,1)} async-done(((bf16[2048,3,1024]{2,0,1:T(8,128)(2,1)}), bf16[8192,3,1024]{2,0,1:T(8,128)(2,1)}) %all-gather.6.cloned.1.call-update) | async-done | bytes 50331664 | tf_op jit(solution)/shard_map/all_gather | solution.py:41
  389.7 0.0 copy-done.3
  389.7 21.9 %fusion.4 = f32[256,3,1024]{2,0,1:T(8,128)S(1)} fusion(bf16[8192,3,1024]{2,0,1:T(8,128)(2,1)} %all-gather.6.cloned.1.call-done, bf16[256,8192]{1,0:T(8,128)(2,1)} %all-gather.4.cloned.1.call-done, f32[8192]{0:T(1024)S(1)} %copy-done.3, f32[256]{0:T(256)S(1)} %add_rsqrt_fusion), kind=kOutput, calls=%fused_computation.6 | convolution fusion | flops 12893290496 | bytes 57705472 | tf_op jit(solution)/shard_map/td,dgc->tgc/dot_general | solution.py:38
  411.6 0.1 fusion.8
  411.8 0.1 slice_bitcast_fusion.1
  411.8 2.4 collective-permute-start
  414.2 0.1 fusion.17
  414.3 0.8 collective-permute-done
  415.1 0.0 copy-done
  415.2 1.0 pad_maximum_fusion
  416.2 2.3 copy.11
  418.5 0.0 copy-start.2
  418.5 17.3 %fusion.11 = f32[64,16,256]{2,1,0:T(8,128)} fusion(bf16[383,64,16]{0,2,1:T(8,128)(2,1)} %bitcast.28, f32[64,256,383]{2,1,0:T(8,128)} %reshape.33), kind=kOutput, calls=%fused_computation.21 | convolution fusion | flops 1204813824 | bytes 26933248 | tf_op jit(solution)/shard_map/gsj,jgi->sgi/dot_general | solution.py:56
  435.8 2.5 copy.12
  438.3 0.0 copy-done.2
  438.3 2.4 fusion.10
  440.7 0.0 all-gather.8.cloned.1.call-update
  440.8 50.5 %all-gather.8.cloned.1.call-done = bf16[256,4096]{1,0:T(8,128)(2,1)} async-done(((bf16[256,1024]{1,0:T(8,128)(2,1)}), bf16[256,4096]{1,0:T(8,128)(2,1)}) %all-gather.8.cloned.1.call-update) | async-done | bytes 2097168 | tf_op jit(solution)/shard_map/all_gather | solution.py:67
  491.2 11.9 %convolution_convert_fusion = bf16[256,2048]{1,0:T(8,128)(2,1)} fusion(bf16[256,4096]{1,0:T(8,128)(2,1)} %all-gather.8.cloned.1.call-done, bf16[4096,2048]{1,0:T(8,128)(2,1)} %param.15), kind=kOutput, calls=%fused_computation.9 | convolution fusion | flops 4295491584 | bytes 19922944 | tf_op jit(solution)/shard_map/dot_general | solution.py:66
  (5 shorter events, 0.1 us)
Async XLA Ops:
  6.5 1.5 copy-start.4
  6.5 1.6 copy-start.1
  6.5 85.9 %all-gather.4.cloned.1.call-start = ((), (), s32[]{:S(2)}) async-start(), calls=%async_computation | async-start | bytes 5242880 | tf_op jit(solution)/shard_map/all_gather | solution.py:34
  7.3 382.4 %all-gather.6.cloned.1.call-start = ((), (), s32[]{:S(2)}) async-start(), calls=%async_computation.1 | async-start | bytes 62914560 | tf_op jit(solution)/shard_map/all_gather | solution.py:41
  8.0 483.2 %all-gather.8.cloned.1.call-start = ((), (), s32[]{:S(2)}) async-start(), calls=%async_computation.2 | async-start | bytes 2621440 | tf_op jit(solution)/shard_map/all_gather | solution.py:67
  49.3 340.4 %copy-start.3 = (f32[8192]{0:T(1024)S(1)}, f32[8192]{0:T(1024)}, u32[]{:S(2)}) copy-start(f32[8192]{0:T(1024)} %param.9) | copy-start | bytes 98308
  95.5 319.6 %copy-start = (bf16[127,1024]{1,0:T(8,128)(2,1)S(1)}, bf16[127,1024]{1,0:T(8,128)(2,1)}, u32[]{:S(2)}) copy-start(bf16[127,1024]{1,0:T(8,128)(2,1)} %param.14) | copy-start | bytes 780292
  411.8 3.3 collective-permute-start
  418.5 19.8 %copy-start.2 = (f32[1024]{0:T(1024)S(1)}, f32[1024]{0:T(1024)}, u32[]{:S(2)}) copy-start(f32[1024]{0:T(1024)} %param.13) | copy-start | bytes 12292
Sparse Core Ops, SparseCore 0:
  8.9 83.4 all-gather.3
  94.0 295.6 all-gather.5
  440.9 50.3 all-gather.7
where the time goes:
time: 510 us
  waiting for transfers between devices  357 us (70%)
  local copies, waits for them, and re-layouts  78.8 us (15%)
  matrix products  51.1 us (10%)
  between operations  13.2 us (3%)
  other arithmetic  6.97 us (1%)
    all_gather x1, waiting for transfers between devices, on_device(): lax.all_gather(weight_in, 'ctx', axis=0, tiled=True)  294 us
    all_gather x1, waiting for transfers between devices, on_device(): lax.all_gather(gated, 'tensor', axis=1, tiled=True)  50.5 us
    reshape x1, local copies, waits for them, and re-layouts, banded_taps(): repeated[:, :shard_rows * width].reshape(group_count, shard_rows, width)  32.8 us
    unnamed x11, local copies, waits for them, and re-layouts  22.1 us
    dot_general x1, matrix products, on_device(): jnp.einsum('td,dgc->tgc', normed, lax.all_gather(weight_in, 'ctx', axis=0...  21.9 us
    dot_general x1, matrix products, on_device(): jnp.einsum('gsj,jgi->sgi', band, grouped, precision=lax.Precision.HIGHEST...  17.3 us
    dot_general x1, matrix products, on_device(): jnp.dot(lax.all_gather(gated, 'tensor', axis=1, tiled=True), output_weigh...  11.9 us
    another operation x1, local copies, waits for them, and re-layouts, banded_taps(): repeated = jnp.tile(first_row, (1, shard_rows))  10.3 us
  transfers between devices with their start and end apart: 4, of which 4 were waited for; matrix products, arithmetic and copies ran while one was open for 15% of the time, Pallas kernels for 0%

commit v1 on v0

--- a/solution.py
+++ b/solution.py
@@ -4,6 +4,17 @@
 from jax.sharding import PartitionSpec as P
 
 GROUP = 16
+
+
+def gather_by_hops(x, mesh_axis, dim):
+    peers = lax.axis_size(mesh_axis)
+    hops = [(i, (i + 1) % peers) for i in range(peers)]
+    shards = [x]
+    for far in range(1, peers):
+        shards = [lax.ppermute(shards[0], mesh_axis, hops), *shards]
+    full = jnp.concatenate(shards, axis=dim)
+    turn = (lax.axis_index(mesh_axis) + 1) * shards[-1].shape[dim]
+    return jnp.roll(full, turn, axis=dim)
 
 
 def passed_along(value, axis, steps):
@@ -31,7 +42,7 @@
 def on_device(
     hidden_in, norm_gain, weight_in, filter_taps, filter_decay, skip_gain, tail_cache, output_weight
 ):
-    gathered = lax.all_gather(hidden_in, "tensor", axis=0, tiled=True)
+    gathered = gather_by_hops(hidden_in, "tensor", 0)
     normed = normalize_rows(gathered, norm_gain)
     shard_rows = normed.shape[0]
     channels = weight_in.shape[2]

time: 510 us -> 430 us (0.84)
  waiting for transfers between devices: 357 us -> 269 us
  local copies, waits for them, and re-layouts: 78.8 us -> 85.6 us
    all_gather x1, waiting for transfers between devices: 294 us -> 165 us  [on_device(): lax.all_gather(weight_in, 'ctx', axis=0, tiled=True)]
    ppermute x0 -> x3, waiting for transfers between devices: none -> 51.3 us  [gather_by_hops(): shards = [lax.ppermute(shards[0], mesh_axis, hops), *shards]]
    all_gather x1 -> x0, waiting for transfers between devices: 10.3 us -> none  [on_device(): gathered = lax.all_gather(hidden_in, 'tensor', axis=0, tiled=True)]
    unnamed x11 -> x22, local copies, waits for them, and re-layouts: 22.1 us -> 28.6 us
  transfers between devices with their start and end apart: 4 -> 6, of which waited for: 4 -> 5; matrix products, arithmetic and copies ran while one was open for 15% -> 18% of each run, Pallas kernels for 0% -> 0%
where the time goes in v1:
time: 430 us; the launch traced here: 429 us
  waiting for transfers between devices  269 us (63%)
  local copies, waits for them, and re-layouts  85.6 us (20%)
  matrix products  51.1 us (12%)
  between operations  13.6 us (3%)
  starting transfers between devices  5.46 us (1%)
  other arithmetic  4.78 us (1%)
    all_gather x1, waiting for transfers between devices, on_device(): lax.all_gather(weight_in, 'ctx', axis=0, tiled=True)  165 us
    ppermute x3, waiting for transfers between devices, gather_by_hops(): shards = [lax.ppermute(shards[0], mesh_axis, hops), *shards]  51.3 us
    all_gather x1, waiting for transfers between devices, on_device(): lax.all_gather(gated, 'tensor', axis=1, tiled=True)  50.5 us
    reshape x1, local copies, waits for them, and re-layouts, banded_taps(): repeated[:, :shard_rows * width].reshape(group_count, shard_rows, width)  33 us
    unnamed x22, local copies, waits for them, and re-layouts  28.6 us
    dot_general x1, matrix products, on_device(): jnp.einsum('td,dgc->tgc', normed, lax.all_gather(weight_in, 'ctx', axis=0...  21.9 us
    dot_general x1, matrix products, on_device(): jnp.einsum('gsj,jgi->sgi', band, grouped, precision=lax.Precision.HIGHEST...  17.3 us
    dot_general x1, matrix products, on_device(): jnp.dot(lax.all_gather(gated, 'tensor', axis=1, tiled=True), output_weigh...  11.9 us
  transfers between devices with their start and end apart: 6, of which 5 were waited for; matrix products, arithmetic and copies ran while one was open for 18% of the time, Pallas kernels for 0%

profile of v1, /device:TPU:0, one launch (start us, length us, event | category | flops | bytes accessed | tf_op | source)
XLA Modules:
  0.0 429.3 jit_solution(16403634156878345419)
XLA Ops:
  6.5 0.0 copy-start
  6.5 0.0 copy-start.6
  6.5 0.0 copy-start.3
  6.5 0.0 all-gather.3.cloned.1.call-start
  6.5 0.7 all-gather.3.cloned.1.call-update
  7.3 0.0 all-gather.5.cloned.1.call-start
  7.3 0.5 copy-done
  7.8 3.0 collective-permute-start
  10.8 25.2 %collective-permute-done = bf16[64,8192]{1,0:T(8,128)(2,1)S(1)} collective-permute-done((bf16[64,8192]{1,0:T(8,128)(2,1)S(1)}, bf16[64,8192]{1,0:T(8,128)(2,1)S(1)}, u32[]{:S(2)}, u32[]{:S(2)}) %collective-permute-start) | collective-permute-done | bytes 1048608 | tf_op jit(solution)/shard_map/ppermute | solution.py:14
  36.0 0.0 collective-permute-start.1
  36.0 26.1 %collective-permute-done.1 = bf16[64,8192]{1,0:T(8,128)(2,1)S(1)} collective-permute-done((bf16[64,8192]{1,0:T(8,128)(2,1)S(1)}, bf16[64,8192]{1,0:T(8,128)(2,1)S(1)}, u32[]{:S(2)}, u32[]{:S(2)}) %collective-permute-start.1) | collective-permute-done | bytes 1048608 | tf_op jit(solution)/shard_map/ppermute | solution.py:14
  62.1 0.0 collective-permute-start.2
  62.1 0.0 copy-done.6
  62.1 0.0 copy-done.3
  62.1 0.1 exponential_multiply_fusion
  62.2 0.1 rev.3
  62.3 10.4 %tile.4 = f32[64,256,384]{2,1,0:T(8,128)} broadcast(f32[64,384]{1,0:T(8,128)S(1)} %concatenate.14), dimensions={0,2} | broadcast | bytes 25264128 | tf_op jit(solution)/shard_map/tile | solution.py:38
  72.8 21.7 %copy.13 = f32[8,8,256,384]{3,1,2,0:T(8,128)S(1)} copy(f32[8,8,256,384]{3,2,1,0:T(8,128)} %bitcast.25) | data formatting | bytes 50331648
  94.5 8.6 %slice.28 = f32[64,98048]{1,0:T(8,128)} slice(f32[64,98304]{1,0:T(8,128)S(1)} %bitcast.26), slice={[0:64], [0:98048]} | slice | bytes 50200576 | tf_op jit(solution)/shard_map/slice | solution.py:39
  103.1 33.0 %reshape.33 = f32[64,256,383]{2,1,0:T(8,128)} reshape(f32[64,98048]{1,0:T(8,128)} %slice.28) | data formatting | bytes 50200576 | tf_op jit(solution)/shard_map/reshape | solution.py:39
  136.1 0.0 collective-permute-done.2
  136.1 1.3 constant_dynamic-update-slice_fusion.7
  137.4 0.1 constant_dynamic-update-slice_fusion.6
  137.4 0.0 copy-start.5
  137.5 0.1 constant_dynamic-update-slice_fusion.5
  137.5 0.1 constant_dynamic-update-slice_fusion.4
  137.6 1.4 constant_dynamic-update-slice_fusion.3
  139.0 0.1 constant_dynamic-update-slice_fusion.2
  139.1 0.1 constant_dynamic-update-slice_fusion.1
  139.2 0.1 constant_dynamic-update-slice_fusion
  139.2 0.0 copy-start.1
  139.3 3.3 copy-done.1
  142.6 0.9 fusion
  143.5 0.0 copy-start.2
  143.5 165.3 %all-gather.3.cloned.1.call-done = bf16[8192,3,1024]{2,0,1:T(8,128)(2,1)} async-done(((bf16[2048,3,1024]{2,0,1:T(8,128)(2,1)}), bf16[8192,3,1024]{2,0,1:T(8,128)(2,1)}) %all-gather.3.cloned.1.call-update) | async-done | bytes 50331664 | tf_op jit(solution)/shard_map/all_gather | solution.py:52
  308.8 0.0 copy-done.5
  308.8 21.9 %fusion.4 = f32[256,3,1024]{2,0,1:T(8,128)S(1)} fusion(bf16[8192,3,1024]{2,0,1:T(8,128)(2,1)} %all-gather.3.cloned.1.call-done, f32[8192]{0:T(1024)S(1)} %copy-done.5, f32[256]{0:T(256)S(1)} %add_rsqrt_fusion, bf16[512,8192]{1,0:T(8,128)(2,1)} %copy-done.1, s32[]{:T(128)S(6)} %select_n.22), kind=kOutput, calls=%fused_computation.6 | convolution fusion | flops 12893290496 | bytes 57705476 | tf_op jit(solution)/shard_map/td,dgc->tgc/dot_general | solution.py:49
  330.7 0.1 fusion.9
  330.9 0.1 slice_bitcast_fusion.1
  330.9 2.4 collective-permute-start.3
  333.3 0.1 fusion.19
  333.5 1.0 collective-permute-done.3
  334.5 0.0 copy-done.2
  334.5 1.0 pad_maximum_fusion
  335.5 2.3 copy.11
  337.8 0.0 copy-start.4
  337.8 17.3 %fusion.13 = f32[64,16,256]{2,1,0:T(8,128)} fusion(bf16[383,64,16]{0,2,1:T(8,128)(2,1)} %bitcast.28, f32[64,256,383]{2,1,0:T(8,128)} %reshape.33), kind=kOutput, calls=%fused_computation.31 | convolution fusion | flops 1204813824 | bytes 26933248 | tf_op jit(solution)/shard_map/gsj,jgi->sgi/dot_general | solution.py:67
  355.1 2.5 copy.12
  357.6 0.0 copy-done.4
  357.6 2.4 fusion.11
  360.1 0.0 all-gather.5.cloned.1.call-update
  360.1 50.5 %all-gather.5.cloned.1.call-done = bf16[256,4096]{1,0:T(8,128)(2,1)} async-done(((bf16[256,1024]{1,0:T(8,128)(2,1)}), bf16[256,4096]{1,0:T(8,128)(2,1)}) %all-gather.5.cloned.1.call-update) | async-done | bytes 2097168 | tf_op jit(solution)/shard_map/all_gather | solution.py:78
  410.6 11.9 %convolution_convert_fusion = bf16[256,2048]{1,0:T(8,128)(2,1)} fusion(bf16[256,4096]{1,0:T(8,128)(2,1)} %all-gather.5.cloned.1.call-done, bf16[4096,2048]{1,0:T(8,128)(2,1)} %param.15), kind=kOutput, calls=%fused_computation.10 | convolution fusion | flops 4295491584 | bytes 19922944 | tf_op jit(solution)/shard_map/dot_general | solution.py:77
  (5 shorter events, 0.1 us)
Async XLA Ops:
  6.5 1.2 copy-start
  6.5 55.6 %copy-start.6 = (f32[64]{0:T(128)S(1)}, f32[64]{0:T(128)}, u32[]{:S(2)}) copy-start(f32[64]{0:T(128)} %param.12) | copy-start | bytes 772
  6.5 55.6 %copy-start.3 = (f32[64,128]{1,0:T(8,128)S(1)}, f32[64,128]{1,0:T(8,128)}, u32[]{:S(2)}) copy-start(f32[64,128]{1,0:T(8,128)} %param.11) | copy-start | bytes 98308
  6.5 302.2 %all-gather.3.cloned.1.call-start = ((), (), s32[]{:S(2)}) async-start(), calls=%async_computation | async-start | bytes 62914560 | tf_op jit(solution)/shard_map/all_gather | solution.py:52
  7.3 403.3 %all-gather.5.cloned.1.call-start = ((), (), s32[]{:S(2)}) async-start(), calls=%async_computation.1 | async-start | bytes 2621440 | tf_op jit(solution)/shard_map/all_gather | solution.py:78
  7.8 28.2 %collective-permute-start = (bf16[64,8192]{1,0:T(8,128)(2,1)S(1)}, bf16[64,8192]{1,0:T(8,128)(2,1)S(1)}, u32[]{:S(2)}, u32[]{:S(2)}) collective-permute-start(bf16[64,8192]{1,0:T(8,128)(2,1)S(1)} %copy-done), channel_id=1, source_target_pairs={{0,4},{4,8},{8,12},{12,0},{1,5},{5,9},{9,13},{13,1},{2,6},{6,10},{... | collective-permute-start | bytes 3145736 | tf_op jit(solution)/shard_map/ppermute | solution.py:14
  36.0 26.1 %collective-permute-start.1 = (bf16[64,8192]{1,0:T(8,128)(2,1)S(1)}, bf16[64,8192]{1,0:T(8,128)(2,1)S(1)}, u32[]{:S(2)}, u32[]{:S(2)}) collective-permute-start(bf16[64,8192]{1,0:T(8,128)(2,1)S(1)} %collective-permute-done), channel_id=1, source_target_pairs={{0,4},{4,8},{8,12},{12,0},{1,5},{5,9},{9,13},{13,1},{2,6},{6,10},{... | collective-permute-start | bytes 3145736 | tf_op jit(solution)/shard_map/ppermute | solution.py:14
  62.1 74.0 %collective-permute-start.2 = (bf16[64,8192]{1,0:T(8,128)(2,1)S(1)}, bf16[64,8192]{1,0:T(8,128)(2,1)}, u32[]{:S(2)}, u32[]{:S(2)}) collective-permute-start(bf16[64,8192]{1,0:T(8,128)(2,1)S(1)} %collective-permute-done.1), channel_id=1, source_target_pairs={{0,4},{4,8},{8,12},{12,0},{1,5},{5,9},{9,13},{13,1},{2,6},{6,10},{... | collective-permute-start | bytes 3145736 | tf_op jit(solution)/shard_map/ppermute | solution.py:14
  137.4 171.3 %copy-start.5 = (f32[8192]{0:T(1024)S(1)}, f32[8192]{0:T(1024)}, u32[]{:S(2)}) copy-start(f32[8192]{0:T(1024)} %param.9) | copy-start | bytes 98308
  139.2 3.3 copy-start.1
  143.5 191.0 %copy-start.2 = (bf16[127,1024]{1,0:T(8,128)(2,1)S(1)}, bf16[127,1024]{1,0:T(8,128)(2,1)}, u32[]{:S(2)}) copy-start(bf16[127,1024]{1,0:T(8,128)(2,1)} %param.14) | copy-start | bytes 780292
  330.9 3.5 collective-permute-start.3
  337.8 19.8 %copy-start.4 = (f32[1024]{0:T(1024)S(1)}, f32[1024]{0:T(1024)}, u32[]{:S(2)}) copy-start(f32[1024]{0:T(1024)} %param.13) | copy-start | bytes 12292
Sparse Core Ops, SparseCore 0:
  8.9 299.8 all-gather.2
  360.2 50.3 all-gather.4
